TPU v7x, 1024 devices: a whole 4x4x32 slice. The times are simulated.
1024 devices in a mesh: ctx: 128 (over z, x), tp: 8 (over y, core).
Axes of the slice: x: 4, y: 4, z: 32, core: 2. Of those that a mesh axis runs over, the one named last changes fastest.
Arguments:
- q_proj: bfloat16 [16384, 8192], P('ctx', 'tp'), may hold values from -110 to 110, as said below
- k_proj: bfloat16 [16384, 8192], P('ctx', 'tp'), may hold values from -6 to 6
- v_proj: bfloat16 [16384, 8192], P('ctx', 'tp'), may hold values from -6 to 6
- cotangent: bfloat16 [16384, 8192], P('ctx', 'tp'), may hold values from -6 to 6
- filters: float32 [128, 8192], P(None, 'tp'), may hold values from -0.5 to 0.5
- gain: float32 [8192], P('tp'), may hold values from 0.5 to 1.5
Outputs:
- grad_q: bfloat16 [16384, 8192], P('ctx', 'tp')
- grad_k: bfloat16 [16384, 8192], P('ctx', 'tp')
- grad_v: bfloat16 [16384, 8192], P('ctx', 'tp')
- grad_filters: float32 [128, 8192], P(None, 'tp')
- grad_gain: float32 [8192], P('tp')
Inputs may be any that keep to these rules, and one draw needn't show every extreme that they name: q_proj has entries of varying magnitude.
All inputs are finite; a program needn't handle non-finite values.
Results may differ from a plain program's by a relative error of at most 0.0049.
Values may be sent and summed in bfloat16 or wider, within the bound.
No kernel may reach another device: no remote copies, remote signals or barrier semaphores. Data moves between devices by JAX's collectives and lax.ppermute only.
A program may use at most 32 MiB of HBM per device.

v0:
```python
import jax
import jax.numpy as jnp
from jax import lax
from jax.sharding import PartitionSpec as P

D = 8192


epsilon = 1e-06


def passed_along(value, axis, by):
    length = lax.axis_size(axis)
    pairs = [(i, i + by) for i in range(length) if 0 <= i + by < length]
    return lax.ppermute(value, axis, pairs)


def depthwise(signal, kernel):
    return lax.conv_general_dilated(
        signal[None],
        kernel[:, None, :],
        (1,),
        "VALID",
        dimension_numbers=("NWC", "WIO", "NWC"),
        feature_group_count=signal.shape[1],
        precision=lax.Precision.HIGHEST,
    )[0]


def shards(q_proj, k_proj, v_proj, cotangent, filters, gain):
    tap_count = filters.shape[0]
    rim_rows = tap_count - 1
    tok_rows = q_proj.shape[0]
    mixed = (k_proj.astype(jnp.float32) * v_proj.astype(jnp.float32)).astype(jnp.bfloat16)
    earlier = passed_along(mixed[tok_rows - rim_rows :], "ctx", 1)
    mixed_ext = jnp.concatenate([earlier, mixed], 0).astype(jnp.float32)
    flipped = filters[::-1]
    conv_fwd = depthwise(mixed_ext, flipped)
    query_f32 = q_proj.astype(jnp.float32)
    cot_f32 = cotangent.astype(jnp.float32)
    product = query_f32 * conv_fwd
    weighted = gain * cot_f32
    sum_squares, sum_cross = lax.psum(
        (jnp.sum(product * product, 1), jnp.sum(weighted * product, 1)), "tp"
    )
    rms = jnp.sqrt(sum_squares / D + epsilon)[:, None]
    cross = sum_cross[:, None]
    grad_product = weighted / rms - product * cross / (D * rms**3)
    grad_conv_all = (query_f32 * grad_product).astype(jnp.bfloat16)
    later = passed_along(grad_conv_all[:rim_rows], "ctx", -1)
    conv_ext = jnp.concatenate([grad_conv_all, later], 0)
    own_conv = conv_ext[:tok_rows]
    grad_q = (grad_product[:tok_rows] * conv_fwd).astype(jnp.bfloat16)
    grad_mixed = depthwise(conv_ext.astype(jnp.float32), filters)
    grad_k = (grad_mixed * v_proj.astype(jnp.float32)).astype(jnp.bfloat16)
    grad_v = (grad_mixed * k_proj.astype(jnp.float32)).astype(jnp.bfloat16)
    local_filters = depthwise(mixed_ext, own_conv.astype(jnp.float32))[::-1]
    local_gain = jnp.sum(cot_f32 * product[:tok_rows] / rms[:tok_rows], 0)
    grad_filters, grad_gain = lax.psum((local_filters, local_gain), "ctx")
    return (grad_q, grad_k, grad_v, grad_filters, grad_gain)


def solution(mesh):
    in_specs = (
        P("ctx", "tp"),
        P("ctx", "tp"),
        P("ctx", "tp"),
        P("ctx", "tp"),
        P(None, "tp"),
        P("tp"),
    )
    out_specs = (P("ctx", "tp"), P("ctx", "tp"), P("ctx", "tp"), P(None, "tp"), P("tp"))
    return jax.shard_map(shards, mesh=mesh, in_specs=in_specs, out_specs=out_specs, check_vma=False)
```

profile of v0, /device:TPU:8, one launch (start us, length us, event | category | flops | bytes accessed | tf_op | source)
XLA Modules:
  0.0 590.7 jit_solution(101638413977309900)
XLA Ops:
  7.2 0.0 all-reduce.2.cloned.1.call-start
  7.2 1.1 fusion.13
  8.4 0.1 slice.8
  8.4 3.4 collective-permute-start
  11.9 0.2 rev.6
  12.1 5.3 collective-permute-done
  17.4 0.1 maximum_bitcast_fusion
  17.5 5.8 fusion.4
  23.3 0.2 multiply_reduce_fusion
  23.5 18.2 %psum.28 = f32[128]{0:T(128)S(1)} all-reduce(f32[128]{0:T(128)S(1)} %multiply_reduce_fusion), channel_id=1, replica_groups=mesh['ctx'=128,'tp'=8] {'tp'}, use_global_device_ids=true, to_apply=%region_1.0 | all-reduce | flops 128 | bytes 1024 | tf_op jit(solution)/shard_map/psum | solution.py:43
  41.7 0.2 fusion.19
  42.0 12.9 %psum.29 = f32[128]{0:T(128)S(1)} all-reduce(f32[128]{0:T(128)S(1)} %get-tuple-element.6), channel_id=1, replica_groups=mesh['ctx'=128,'tp'=8] {'tp'}, use_global_device_ids=true, to_apply=%region_3.0 | all-reduce | flops 128 | bytes 1024 | tf_op jit(solution)/shard_map/psum | solution.py:43
  54.9 0.3 fusion.11
  55.2 1.3 collective-permute-start.1
  56.5 7.3 %fusion.2 = f32[1,128,1024]{2,0,1:T(1,128)S(1)} fusion(bf16[1,255,1024]{2,1,0:T(8,128)(2,1)S(1)} %maximum_bitcast_fusion, bf16[128,1,1024]{2,0,1:T(8,128)(2,1)S(1)} %bitcast.30), kind=kOutput, calls=%fused_computation.2 | convolution fusion | flops 33554432 | bytes 1308672 | tf_op jit(solution)/shard_map/conv_general_dilated | solution.py:19
  63.8 0.1 copy.50
  63.9 2.6 rev.7
  66.5 0.0 all-reduce.2.cloned.1.call-update
  66.6 288.9 %psum.31 = f32[1024]{0:T(1024)} all-reduce(f32[1024]{0:T(1024)S(1)} %get-tuple-element.5), channel_id=1, replica_groups=mesh['ctx'=128,'tp'=8] {'ctx'}, use_global_device_ids=true, to_apply=%region_6.0 | all-reduce | flops 1024 | bytes 8192 | tf_op jit(solution)/shard_map/psum | solution.py:59
  355.5 0.8 fusion.15
  356.4 5.8 fusion
  362.2 1.0 fusion.12
  363.2 218.8 %all-reduce.2.cloned.1.call-done = f32[128,1024]{1,0:T(8,128)} async-done(((f32[128,1024]{1,0:T(8,128)}), f32[128,1024]{1,0:T(8,128)}) %all-reduce.2.cloned.1.call-update) | async-done | bytes 524304 | tf_op jit(solution)/shard_map/psum | solution.py:59
  582.0 1.9 copy.52
  (15 shorter events, 0.1 us)
Async XLA Ops:
  7.2 4.7 copy-start.4
  7.2 574.8 %all-reduce.2.cloned.1.call-start = ((), (), s32[]{:S(2)}) async-start(), calls=%async_computation | async-start | bytes 1048576 | tf_op jit(solution)/shard_map/psum | solution.py:59
  8.4 8.9 %collective-permute-start = (bf16[127,1024]{1,0:T(8,128)(2,1)S(1)}, bf16[127,1024]{1,0:T(8,128)(2,1)S(1)}, u32[]{:S(2)}, u32[]{:S(2)}) collective-permute-start(bf16[127,1024]{1,0:T(8,128)(2,1)S(1)} %slice.8), channel_id=1, source_target_pairs={{0,8},{8,16},{16,24},{24,32},{32,40},{40,48},{48,56},{56,64},{64,7... | collective-permute-start | bytes 780296 | tf_op jit(solution)/shard_map/ppermute | solution.py:15
  17.5 5.8 copy-start
  23.3 18.4 %copy-start.3 = (bf16[128,1024]{1,0:T(8,128)(2,1)S(1)}, bf16[128,1024]{1,0:T(8,128)(2,1)}, u32[]{:S(2)}) copy-start(bf16[128,1024]{1,0:T(8,128)(2,1)} %param.9) | copy-start | bytes 786436
  23.5 18.3 %copy-start.5 = (f32[1024]{0:T(1024)S(1)}, f32[1024]{0:T(1024)}, u32[]{:S(2)}) copy-start(f32[1024]{0:T(1024)} %param.11) | copy-start | bytes 12292
  55.2 301.2 %collective-permute-start.1 = (bf16[127,1024]{1,0:T(8,128)(2,1)S(1)}, bf16[127,1024]{1,0:T(8,128)(2,1)S(1)}, u32[]{:S(2)}, u32[]{:S(2)}) collective-permute-start(bf16[127,1024]{1,0:T(8,128)(2,1)S(1)} %bitcast.29), channel_id=1, source_target_pairs={{8,0},{16,8},{24,16},{32,24},{40,32},{48,40},{56,48},{64,56},{72,6... | collective-permute-start | bytes 780296 | tf_op jit(solution)/shard_map/ppermute | solution.py:15
  356.4 5.8 copy-start.1
  356.4 5.8 copy-start.2
Sparse Core Ops, SparseCore 0:
  66.7 515.2 all-reduce.1
where the time goes:
time: 591 us
  blocking collectives  320 us (54%)
  waiting for transfers between devices  224 us (38%)
  matrix products  18.9 us (3%)
  between operations  14.2 us (2%)
    psum x1, blocking collectives, shards(): grad_filters, grad_gain = lax.psum((local_filters, local_gain), 'ctx')  289 us
    psum x1, waiting for transfers between devices, shards(): grad_filters, grad_gain = lax.psum((local_filters, local_gain), 'ctx')  219 us
    psum x2, blocking collectives, shards(): lax.psum((jnp.sum(product * product, 1), jnp.sum(weighted * product, 1)),...  31.2 us
    conv_general_dilated x3, matrix products, depthwise(): lax.conv_general_dilated(signal[None], kernel[:, None, :], (1,), 'VALID',...  18.9 us
  transfers between devices with their start and end apart: 3, of which 2 were waited for; matrix products, arithmetic and copies ran while one was open for 3% of the time, Pallas kernels for 0%

commit v1 on v0

v1 whole, which is shorter than its diff:
```python
import jax
import jax.numpy as jnp
from jax import lax
from jax.sharding import Mesh, PartitionSpec as P

D = 8192
CTX = ("zh", "zl", "x")
NEAR = ("zl", "x")
FAR = "zh"

epsilon = 1e-06


def passed_along(value, by):
    length = lax.axis_size(CTX)
    pairs = [(i, i + by) for i in range(length) if 0 <= i + by < length]
    return lax.ppermute(value, CTX, pairs)


def shared(value, axes):
    size = lax.axis_size(axes)
    copies = jnp.broadcast_to(value[None], (size, *value.shape))
    return lax.all_to_all(copies, axes, 0, 0)


def depthwise(signal, kernel):
    return lax.conv_general_dilated(
        signal[None],
        kernel[:, None, :],
        (1,),
        "VALID",
        dimension_numbers=("NWC", "WIO", "NWC"),
        feature_group_count=signal.shape[1],
        precision=lax.Precision.HIGHEST,
    )[0]


def token_sums(local_filters, local_gain):
    taps, width = local_filters.shape
    near = lax.axis_size(NEAR)
    rows = taps // near
    parts = local_gain.reshape(width // 128, 1, 128)
    parts = jnp.pad(parts, ((0, near - width // 128), (0, rows - 1), (0, 0))).reshape(taps, 128)
    block = jnp.concatenate([local_filters, parts], 1).reshape(near, rows, width + 128)
    own = lax.all_to_all(block.astype(jnp.bfloat16), NEAR, 0, 0)
    own = jnp.sum(own.astype(jnp.float32), 0)
    own = shared(own.astype(jnp.bfloat16), FAR)
    own = jnp.sum(own.astype(jnp.float32), 0)
    whole = shared(own.astype(jnp.bfloat16), NEAR).astype(jnp.float32)
    grad_filters = whole[:, :, :width].reshape(taps, width)
    grad_gain = whole[: width // 128, 0, width:].reshape(width)
    return grad_filters, grad_gain


def shards(q_proj, k_proj, v_proj, cotangent, filters, gain):
    tap_count = filters.shape[0]
    rim_rows = tap_count - 1
    tok_rows = q_proj.shape[0]
    mixed = (k_proj.astype(jnp.float32) * v_proj.astype(jnp.float32)).astype(jnp.bfloat16)
    earlier = passed_along(mixed, 1)
    mixed_ext = jnp.concatenate([earlier, mixed], 0).astype(jnp.float32)[tok_rows - rim_rows :]
    flipped = filters[::-1]
    conv_fwd = depthwise(mixed_ext, flipped)
    query_f32 = q_proj.astype(jnp.float32)
    cot_f32 = cotangent.astype(jnp.float32)
    product = query_f32 * conv_fwd
    weighted = gain * cot_f32
    sums = jnp.stack([jnp.sum(product * product, 1), jnp.sum(weighted * product, 1)])
    sums = jnp.pad(sums, ((0, 6), (0, 0)))
    sum_squares, sum_cross = jnp.sum(shared(sums, "tp"), 0)[:2]
    rms = jnp.sqrt(sum_squares / D + epsilon)[:, None]
    cross = sum_cross[:, None]
    grad_product = weighted / rms - product * cross / (D * rms**3)
    grad_conv = (query_f32 * grad_product).astype(jnp.bfloat16)
    later = passed_along(grad_conv, -1)
    conv_ext = jnp.concatenate([grad_conv, later[:rim_rows]], 0)
    grad_q = (grad_product * conv_fwd).astype(jnp.bfloat16)
    local_filters = depthwise(mixed_ext, grad_conv.astype(jnp.float32))[::-1]
    local_gain = jnp.sum(cot_f32 * product / rms, 0)
    grad_filters, grad_gain = token_sums(local_filters, local_gain)
    grad_mixed = depthwise(conv_ext.astype(jnp.float32), filters)
    grad_k = (grad_mixed * v_proj.astype(jnp.float32)).astype(jnp.bfloat16)
    grad_v = (grad_mixed * k_proj.astype(jnp.float32)).astype(jnp.bfloat16)
    return (grad_q, grad_k, grad_v, grad_filters, grad_gain)


def solution(mesh):
    cube = 4
    far = mesh.devices.shape[0] // (cube * cube)
    split = Mesh(mesh.devices.reshape(far, cube, cube, -1), (*CTX, "tp"))
    rows = P(CTX, "tp")
    in_specs = (rows, rows, rows, rows, P(None, "tp"), P("tp"))
    out_specs = (rows, rows, rows, P(None, "tp"), P("tp"))
    return jax.shard_map(shards, mesh=split, in_specs=in_specs, out_specs=out_specs, check_vma=False)
```

time: 591 us -> 137 us (0.23)
  the two profiles are of different devices: /device:TPU:8 before, /device:TPU:38 now
where the time goes in v1:
time: 137 us
  blocking collectives  81.4 us (59%)
  matrix products  18.9 us (14%)
  waiting for transfers between devices  15.2 us (11%)
  starting transfers between devices  13.9 us (10%)
  other arithmetic  3.88 us (3%)
  local copies, waits for them, and re-layouts  2.9 us (2%)
    all_to_all x2, blocking collectives, shared(): return lax.all_to_all(copies, axes, 0, 0)  63.6 us
    conv_general_dilated x3, matrix products, depthwise(): lax.conv_general_dilated(signal[None], kernel[:, None, :], (1,), 'VALID',...  18.9 us
    all_to_all x1, blocking collectives, token_sums(): own = lax.all_to_all(block.astype(jnp.bfloat16), NEAR, 0, 0)  17.9 us
    ppermute x2, waiting for transfers between devices, passed_along(): return lax.ppermute(value, CTX, pairs)  15.2 us
    all_to_all x1, starting transfers between devices, shared(): return lax.all_to_all(copies, axes, 0, 0)  7.39 us
    ppermute x2, starting transfers between devices, passed_along(): return lax.ppermute(value, CTX, pairs)  6.49 us
  transfers between devices with their start and end apart: 3, of which 2 were waited for; matrix products, arithmetic and copies ran while one was open for 6% of the time, Pallas kernels for 0%

profile of v1, /device:TPU:38, one launch (start us, length us, event | category | flops | bytes accessed | tf_op | source)
XLA Modules:
  0.0 137.1 jit_solution(15199079646071128628)
XLA Ops:
  0.6 1.2 fusion.14
  1.8 3.7 %collective-permute-start = (bf16[128,1024]{1,0:T(8,128)(2,1)S(1)}, bf16[128,1024]{1,0:T(8,128)(2,1)S(1)}, u32[]{:S(2)}, u32[]{:S(2)}) collective-permute-start(bf16[128,1024]{1,0:T(8,128)(2,1)S(1)} %fusion.14), channel_id=1, source_target_pairs={{0,8},{8,16},{16,24},{24,32},{32,40},{40,48},{48,56},{56,64},{64,7... | collective-permute-start | bytes 786440 | tf_op jit(solution)/shard_map/ppermute | solution.py:17
  5.6 0.2 rev.6
  5.8 5.9 %collective-permute-done = bf16[128,1024]{1,0:T(8,128)(2,1)S(1)} collective-permute-done((bf16[128,1024]{1,0:T(8,128)(2,1)S(1)}, bf16[128,1024]{1,0:T(8,128)(2,1)S(1)}, u32[]{:S(2)}, u32[]{:S(2)}) %collective-permute-start) | collective-permute-done | bytes 262176 | tf_op jit(solution)/shard_map/ppermute | solution.py:17
  11.7 0.1 fusion.16
  11.9 0.0 copy-start
  11.9 5.8 %fusion.4 = f32[1,128,1024]{2,0,1:T(1,128)S(1)} fusion(bf16[1,255,1024]{2,1,0:T(8,128)(2,1)S(1)} %fusion.16, f32[128,1,1024]{2,0,1:T(8,128)S(1)} %bitcast.48), kind=kOutput, calls=%fused_computation.4 | convolution fusion | flops 201326592 | bytes 1570816 | tf_op jit(solution)/shard_map/conv_general_dilated | solution.py:27
  17.7 0.2 multiply_reduce_fusion
  18.0 9.7 %all_to_all.20 = f32[8,8,128]{2,1,0:T(8,128)S(1)} all-to-all(f32[8,8,128]{2,1,0:T(8,128)S(1)} %broadcast_in_dim.18), channel_id=1, replica_groups=mesh['zh'=8,'zl'=4,'x'=4,'tp'=8] {'tp'}, dimensions={0} | all-to-all | bytes 65536 | tf_op jit(solution)/shard_map/all_to_all | solution.py:23
  27.7 0.3 fusion.12
  28.1 7.4 %fusion.2 = bf16[1,128,1024]{2,0,1:T(2,128)(2,1)S(1)} fusion(bf16[1,255,1024]{2,1,0:T(8,128)(2,1)S(1)} %fusion.16, bf16[128,1,1024]{2,0,1:T(8,128)(2,1)S(1)} %bitcast.46), kind=kOutput, calls=%fused_computation.2 | convolution fusion | flops 33554432 | bytes 1046528 | tf_op jit(solution)/shard_map/conv_general_dilated | solution.py:27
  35.5 0.1 copy.59
  35.6 0.3 rev.7
  35.9 17.9 %all_to_all.21 = bf16[16,8,1152]{2,1,0:T(8,128)(2,1)S(1)} all-to-all(bf16[16,8,1152]{2,1,0:T(8,128)(2,1)S(1)} %fusion.22), channel_id=1, replica_groups=mesh['zh'=8,'zl'=4,'x'=4,'tp'=8] {'zl','x'}, dimensions={0} | all-to-all | bytes 589824 | tf_op jit(solution)/shard_map/all_to_all | solution.py:45
  53.9 53.8 %all_to_all.22 = bf16[8,8,1152]{2,1,0:T(8,128)(2,1)S(1)} all-to-all(bf16[8,8,1152]{2,1,0:T(8,128)(2,1)S(1)} %broadcast_in_dim.42), channel_id=1, replica_groups=mesh['zh'=8,'zl'=4,'x'=4,'tp'=8] {'zh'}, dimensions={0} | all-to-all | bytes 294912 | tf_op jit(solution)/shard_map/all_to_all | solution.py:23
  107.8 0.7 broadcast_in_dim.43
  108.5 7.4 %all-to-all-start.3 = ((bf16[16,8,1152]{2,1,0:T(8,128)(2,1)}), bf16[16,8,1152]{2,1,0:T(8,128)(2,1)S(1)}, u32[]{:S(2)}, u32[]{:S(2)}) async-start(bf16[16,8,1152]{2,1,0:T(8,128)(2,1)} %broadcast_in_dim.43), calls=%async_computation.3 | async-start | bytes 589824 | tf_op jit(solution)/shard_map/all_to_all | solution.py:23
  115.9 2.8 %collective-permute-start.1 = (bf16[128,1024]{1,0:T(8,128)(2,1)S(1)}, bf16[128,1024]{1,0:T(8,128)(2,1)S(1)}, u32[]{:S(2)}, u32[]{:S(2)}) collective-permute-start(bf16[128,1024]{1,0:T(8,128)(2,1)S(1)} %get-tuple-element.7), channel_id=1, source_target_pairs={{8,0},{16,8},{24,16},{32,24},{40,32},{48,40},{56,48},{64,56},{72,6... | collective-permute-start | bytes 786440 | tf_op jit(solution)/shard_map/ppermute | solution.py:17
  118.7 0.8 fusion.17
  119.5 9.2 %collective-permute-done.1 = bf16[128,1024]{1,0:T(8,128)(2,1)S(1)} collective-permute-done((bf16[128,1024]{1,0:T(8,128)(2,1)S(1)}, bf16[128,1024]{1,0:T(8,128)(2,1)S(1)}, u32[]{:S(2)}, u32[]{:S(2)}) %collective-permute-start.1) | collective-permute-done | bytes 262176 | tf_op jit(solution)/shard_map/ppermute | solution.py:17
  128.8 5.8 %fusion = f32[1,128,1024]{2,0,1:T(1,128)S(1)} fusion(bf16[1,255,1024]{2,1,0:T(8,128)(2,1)S(1)} %maximum_bitcast_fusion, f32[128,1,1024]{2,0,1:T(8,128)S(1)} %bitcast.47), kind=kOutput, calls=%fused_computation | convolution fusion | flops 201326592 | bytes 1570816 | tf_op jit(solution)/shard_map/conv_general_dilated | solution.py:27
  134.6 1.0 fusion.13
  135.6 0.8 slice_bitcast_fusion
  136.5 0.6 slice.21
  (24 shorter events, 0.3 us)
Async XLA Ops:
  0.6 4.9 %copy-start.4 = (f32[128,1024]{1,0:T(8,128)S(1)}, f32[128,1024]{1,0:T(8,128)}, u32[]{:S(2)}) copy-start(f32[128,1024]{1,0:T(8,128)} %param.10) | copy-start | bytes 1572868
  1.8 9.9 %collective-permute-start = (bf16[128,1024]{1,0:T(8,128)(2,1)S(1)}, bf16[128,1024]{1,0:T(8,128)(2,1)S(1)}, u32[]{:S(2)}, u32[]{:S(2)}) collective-permute-start(bf16[128,1024]{1,0:T(8,128)(2,1)S(1)} %fusion.14), channel_id=1, source_target_pairs={{0,8},{8,16},{16,24},{24,32},{32,40},{40,48},{48,56},{56,64},{64,7... | collective-permute-start | bytes 786440 | tf_op jit(solution)/shard_map/ppermute | solution.py:17
  11.9 5.8 %copy-start = (bf16[128,1024]{1,0:T(8,128)(2,1)S(1)}, bf16[128,1024]{1,0:T(8,128)(2,1)}, u32[]{:S(2)}) copy-start(bf16[128,1024]{1,0:T(8,128)(2,1)} %param.6) | copy-start | bytes 786436
  11.9 5.8 %copy-start.1 = (bf16[128,1024]{1,0:T(8,128)(2,1)S(1)}, bf16[128,1024]{1,0:T(8,128)(2,1)}, u32[]{:S(2)}) copy-start(bf16[128,1024]{1,0:T(8,128)(2,1)} %param.9) | copy-start | bytes 786436
  11.9 5.8 %copy-start.5 = (f32[1024]{0:T(1024)S(1)}, f32[1024]{0:T(1024)}, u32[]{:S(2)}) copy-start(f32[1024]{0:T(1024)} %param.11) | copy-start | bytes 12292
  108.5 27.1 %all-to-all-start.3 = ((bf16[16,8,1152]{2,1,0:T(8,128)(2,1)}), bf16[16,8,1152]{2,1,0:T(8,128)(2,1)S(1)}, u32[]{:S(2)}, u32[]{:S(2)}) async-start(bf16[16,8,1152]{2,1,0:T(8,128)(2,1)} %broadcast_in_dim.43), calls=%async_computation.3 | async-start | bytes 589824 | tf_op jit(solution)/shard_map/all_to_all | solution.py:23
  115.9 12.8 %collective-permute-start.1 = (bf16[128,1024]{1,0:T(8,128)(2,1)S(1)}, bf16[128,1024]{1,0:T(8,128)(2,1)S(1)}, u32[]{:S(2)}, u32[]{:S(2)}) collective-permute-start(bf16[128,1024]{1,0:T(8,128)(2,1)S(1)} %get-tuple-element.7), channel_id=1, source_target_pairs={{8,0},{16,8},{24,16},{32,24},{40,32},{48,40},{56,48},{64,56},{72,6... | collective-permute-start | bytes 786440 | tf_op jit(solution)/shard_map/ppermute | solution.py:17
  128.7 5.8 %copy-start.2 = (bf16[128,1024]{1,0:T(8,128)(2,1)S(1)}, bf16[128,1024]{1,0:T(8,128)(2,1)}, u32[]{:S(2)}) copy-start(bf16[128,1024]{1,0:T(8,128)(2,1)} %param.8) | copy-start | bytes 786436
  128.8 5.8 %copy-start.3 = (bf16[128,1024]{1,0:T(8,128)(2,1)S(1)}, bf16[128,1024]{1,0:T(8,128)(2,1)}, u32[]{:S(2)}) copy-start(bf16[128,1024]{1,0:T(8,128)(2,1)} %param.7) | copy-start | bytes 786436

commit v2 on v1

v2 whole, which is shorter than its diff:
```python
import jax
import jax.numpy as jnp
from jax import lax
from jax.experimental import pallas as pl
from jax.experimental.pallas import tpu as pltpu
from jax.sharding import Mesh, PartitionSpec as P

D = 8192
CTX = ("zh", "zl", "x")
NEAR = ("zl", "x")
FAR = "zh"
LANES = 128
SUB = 8
VMEM_BYTES = 8 << 20

epsilon = 1e-06
f32 = jnp.float32
bf16 = jnp.bfloat16


def passed_along(value, by):
    length = lax.axis_size(CTX)
    pairs = [(i, i + by) for i in range(length) if 0 <= i + by < length]
    return lax.ppermute(value, CTX, pairs)


def shared(value, axes):
    size = lax.axis_size(axes)
    copies = jnp.broadcast_to(value[None], (size, *value.shape))
    return lax.all_to_all(copies, axes, 0, 0)


def call(kernel, outs, *operands, scratch=(), name, flops):
    in_vmem = pl.BlockSpec(memory_space=pltpu.VMEM)
    moved = sum(x.size * x.dtype.itemsize for x in (*operands, *outs))
    return pl.pallas_call(
        kernel,
        out_shape=outs,
        in_specs=[in_vmem] * len(operands),
        out_specs=tuple(in_vmem for _ in outs),
        scratch_shapes=list(scratch),
        name=name,
        compiler_params=pltpu.CompilerParams(vmem_limit_bytes=VMEM_BYTES),
        cost_estimate=pl.CostEstimate(flops=flops, bytes_accessed=moved, transcendentals=0),
    )(*operands)


def struct(shape, dtype):
    return jax.ShapeDtypeStruct(shape, dtype)


def over_tiles(width, body):
    def step(tile, carry):
        body(tile, pl.ds(pl.multiple_of(tile * LANES, LANES), LANES))
        return carry

    lax.fori_loop(0, width // LANES, step, 0)


def blocks(value):
    return [value[SUB * i : SUB * i + SUB] for i in range(value.shape[0] // SUB)]


def fill(window, at, value):
    window[pl.ds(at, value.shape[0]), :] = value.astype(f32)


def own_kernel(mixed, filters, conv, window):
    rows, width = mixed.shape
    count = rows // SUB
    window[pl.ds(0, SUB), :] = jnp.zeros((SUB, LANES), f32)

    def tile(_, lanes):
        fill(window, SUB, mixed[:, lanes])
        total = [None] * count
        for shift in range(SUB):
            slid = [window[pl.ds(SUB + SUB * i - shift, SUB), :] for i in range(count)]
            for step in range(count):
                weight = filters[pl.ds(SUB * step + shift, 1), lanes]
                for i in range(step, count):
                    term = weight * slid[i - step]
                    total[i] = term if total[i] is None else total[i] + term
        for i in range(count):
            conv[pl.ds(SUB * i, SUB), lanes] = total[i]

    over_tiles(width, tile)


def rim_kernel(own, earlier, filters, query, cot, gain, conv, sums, window, squares, crosses):
    rows, width = own.shape
    count = rows // SUB
    window[pl.ds(rows, SUB), :] = jnp.zeros((SUB, LANES), f32)
    squares[...] = jnp.zeros(squares.shape, f32)
    crosses[...] = jnp.zeros(crosses.shape, f32)

    def tile(_, lanes):
        fill(window, 0, earlier[:, lanes])
        total = [own[pl.ds(SUB * i, SUB), lanes] for i in range(count)]
        for shift in range(SUB):
            slid = [window[pl.ds(rows - SUB * i - shift, SUB), :] for i in range(count)]
            for step in range(count):
                weight = filters[pl.ds(SUB * step + shift, 1), lanes]
                for i in range(step + 1):
                    total[i] = total[i] + weight * slid[step - i]
        for i in range(count):
            at = pl.ds(SUB * i, SUB)
            conv[at, lanes] = total[i]
        whole = conv[:, lanes]
        product = query[:, lanes].astype(f32) * whole
        weighted = gain[:, lanes] * cot[:, lanes].astype(f32)
        squares[...] += product * product
        crosses[...] += weighted * product

    over_tiles(width, tile)
    square = jnp.sum(squares[...].T, 0, keepdims=True)
    cross = jnp.sum(crosses[...].T, 0, keepdims=True)
    first = lax.broadcasted_iota(jnp.int32, sums.shape[1:], 0) == 0
    both = jnp.where(first, square, cross)
    for i in range(sums.shape[0]):
        sums[i] = both


def gathered(parts):
    row = lax.broadcasted_iota(jnp.int32, (SUB, LANES), 0)
    half = 1
    while half < SUB:
        low = (row & half) == 0
        parts = [
            jnp.where(low, a, b) + pltpu.roll(jnp.where(low, b, a), half, 0)
            for a, b in zip(parts[::2], parts[1::2])
        ]
        half *= 2
    return parts[0]


def grads_kernel(
    sums, conv, query, cot, gain, earlier, mixed, grad_conv, grad_q, block, window, inverse, pull, partial
):
    rows, width = conv.shape
    count = rows // SUB
    both = jnp.sum(sums[...], 0)
    rms = jnp.sqrt(both[0:1] / D + epsilon)
    inverse[...] = jnp.broadcast_to(1.0 / rms, (LANES, rows)).T
    pull[...] = jnp.broadcast_to(both[1:2] / (D * (rms * rms * rms)), (LANES, rows)).T
    block[:, width:] = jnp.zeros((rows, LANES), bf16)

    def tile(index, lanes):
        whole = conv[:, lanes]
        query_f32 = query[:, lanes].astype(f32)
        cot_f32 = cot[:, lanes].astype(f32)
        product = query_f32 * whole
        grad_product = gain[:, lanes] * cot_f32 * inverse[...] - product * pull[...]
        rounded = (query_f32 * grad_product).astype(bf16)
        grad_conv[:, lanes] = rounded
        grad_q[:, lanes] = (grad_product * whole).astype(bf16)
        gains = jnp.sum((cot_f32 * product * inverse[...]).reshape(count, SUB, LANES), 0)
        block[pl.ds(pl.multiple_of(index * SUB, SUB), SUB), width:] = gains.astype(bf16)
        fill(window, 0, earlier[:, lanes])
        fill(window, rows, mixed[:, lanes])
        ours = blocks(rounded.astype(f32))
        for shift in range(SUB):
            slid = [window[pl.ds(SUB * (i + 1) - shift, SUB), :] for i in range(2 * count - 1)]
            for step in range(count):
                terms = [ours[i] * slid[count - 1 + i - step] for i in range(count)]
                while len(terms) > 1:
                    terms = [a + b for a, b in zip(terms[::2], terms[1::2])]
                partial[SUB * step + shift] = terms[0]
        for step in range(0, count, 2):
            pair = [gathered([partial[SUB * s + i] for i in range(SUB)]) for s in (step, step + 1)]
            block[pl.ds(SUB * step, 2 * SUB), lanes] = jnp.concatenate(pair, 0).astype(bf16)

    over_tiles(width, tile)


def back_kernel(grad_conv, later, filters, k_proj, v_proj, grad_k, grad_v, window):
    rows, width = grad_conv.shape
    count = rows // SUB

    def tile(_, lanes):
        fill(window, 0, grad_conv[:, lanes])
        fill(window, rows, later[:, lanes])
        total = [jnp.zeros((SUB, LANES), f32)] * count
        for shift in range(SUB):
            slid = [window[pl.ds(SUB * i + shift, SUB), :] for i in range(2 * count - 1)]
            for step in range(count):
                weight = filters[pl.ds(SUB * step + shift, 1), lanes]
                for i in range(count):
                    total[i] = total[i] + weight * slid[i + step]
        grad_mixed = jnp.concatenate(total, 0)
        grad_k[:, lanes] = (grad_mixed * v_proj[:, lanes].astype(f32)).astype(bf16)
        grad_v[:, lanes] = (grad_mixed * k_proj[:, lanes].astype(f32)).astype(bf16)

    over_tiles(width, tile)


def final_kernel(whole, grad_filters, grad_gain):
    width = grad_filters.shape[1]
    grad_filters[...] = whole[:, :width].astype(f32)
    for i in range(width // LANES):
        part = whole[pl.ds(SUB * i, SUB), width:].astype(f32)
        grad_gain[pl.ds(i, 1), :] = jnp.sum(part, 0, keepdims=True)


def shards(q_proj, k_proj, v_proj, cotangent, filters, gain):
    rows, width = q_proj.shape
    macs = 2 * filters.shape[0] * rows * width
    tile = pltpu.VMEM((rows, LANES), f32)
    short = pltpu.VMEM((rows + SUB, LANES), f32)
    long = pltpu.VMEM((2 * rows, LANES), f32)
    gain = gain.reshape(1, width)
    mixed = (k_proj.astype(f32) * v_proj.astype(f32)).astype(bf16)
    earlier = passed_along(mixed, 1)
    (own,) = call(
        own_kernel, (struct((rows, width), f32),), mixed, filters, scratch=(short,), name="own", flops=macs // 2
    )
    members = lax.axis_size("tp")
    conv, sums = call(
        rim_kernel,
        (struct((rows, width), f32), struct((members, SUB, rows), f32)),
        own,
        earlier,
        filters,
        q_proj,
        cotangent,
        gain,
        scratch=(short, tile, tile),
        name="rim",
        flops=macs // 2,
    )
    sums = lax.all_to_all(sums, "tp", 0, 0)
    grad_conv, grad_q, block = call(
        grads_kernel,
        (struct((rows, width), bf16), struct((rows, width), bf16), struct((rows, width + LANES), bf16)),
        sums,
        conv,
        q_proj,
        cotangent,
        gain,
        earlier,
        mixed,
        scratch=(long, tile, tile, pltpu.VMEM((rows, SUB, LANES), f32)),
        name="grads",
        flops=macs,
    )
    near = lax.axis_size(NEAR)
    block = block.reshape(near, rows // near, width + LANES)
    block = lax.all_to_all(block, NEAR, 0, 0)
    block = jnp.sum(block.astype(f32), 0).astype(bf16)
    block, grad_conv = lax.optimization_barrier((block, grad_conv))
    block = shared(block, FAR)
    later = passed_along(grad_conv, -1)
    grad_k, grad_v = call(
        back_kernel,
        (struct((rows, width), bf16), struct((rows, width), bf16)),
        grad_conv,
        later,
        filters,
        k_proj,
        v_proj,
        scratch=(long,),
        name="back",
        flops=macs,
    )
    block = jnp.sum(block.astype(f32), 0).astype(bf16)
    block, grad_k = lax.optimization_barrier((block, grad_k))
    whole = shared(block, NEAR).reshape(rows, width + LANES)
    grad_filters, grad_gain = call(
        final_kernel,
        (struct((rows, width), f32), struct((width // LANES, LANES), f32)),
        whole,
        name="final",
        flops=0,
    )
    return (grad_q, grad_k, grad_v, grad_filters, grad_gain.reshape(width))


def solution(mesh):
    cube = 4
    far = mesh.devices.shape[0] // (cube * cube)
    split = Mesh(mesh.devices.reshape(far, cube, cube, -1), (*CTX, "tp"))
    rows = P(CTX, "tp")
    in_specs = (rows, rows, rows, rows, P(None, "tp"), P("tp"))
    out_specs = (rows, rows, rows, P(None, "tp"), P("tp"))
    return jax.shard_map(shards, mesh=split, in_specs=in_specs, out_specs=out_specs, check_vma=False)
```

time: 137 us -> 121 us (0.88)
  the two profiles are of different devices: /device:TPU:38 before, /device:TPU:2 now
where the time goes in v2:
time: 121 us
  blocking collectives  35.9 us (30%)
  waiting for transfers between devices  33 us (27%)
  starting transfers between devices  31.9 us (26%)
  Pallas kernels  17 us (14%)
  other arithmetic  1.23 us (1%)
    all_to_all x1, starting transfers between devices, shared(): return lax.all_to_all(copies, axes, 0, 0)  25 us
    ppermute x2, waiting for transfers between devices, passed_along(): return lax.ppermute(value, CTX, pairs)  18.1 us
    pallas_call x5, Pallas kernels, call(): pl.pallas_call(kernel, out_shape=outs, in_specs=[in_vmem] * len(operands)...  17 us
    all_to_all x1, blocking collectives, shared(): return lax.all_to_all(copies, axes, 0, 0)  15.2 us
    all_to_all x1, waiting for transfers between devices, shared(): return lax.all_to_all(copies, axes, 0, 0)  14.9 us
    all_to_all x1, blocking collectives, shards(): block = lax.all_to_all(block, NEAR, 0, 0)  12.9 us
    all_to_all x1, blocking collectives, shards(): sums = lax.all_to_all(sums, 'tp', 0, 0)  7.82 us
    ppermute x2, starting transfers between devices, passed_along(): return lax.ppermute(value, CTX, pairs)  6.88 us
  transfers between devices with their start and end apart: 3, of which 3 were waited for; matrix products, arithmetic and copies ran while one was open for 0% of the time, Pallas kernels for 6%

profile of v2, /device:TPU:2, one launch (start us, length us, event | category | flops | bytes accessed | tf_op | source)
XLA Modules:
  0.0 120.6 jit_solution(2800109087500658587)
XLA Ops:
  0.6 0.0 copy-start
  0.6 1.2 multiply_convert_fusion.mixed
  1.8 0.0 copy-start.1
  1.8 0.0 copy-start.2
  1.8 3.5 %collective-permute-start = (bf16[128,1024]{1,0:T(8,128)(2,1)S(1)}, bf16[128,1024]{1,0:T(8,128)(2,1)S(1)}, u32[]{:S(2)}, u32[]{:S(2)}) collective-permute-start(bf16[128,1024]{1,0:T(8,128)(2,1)S(1)} %multiply_convert_fusion.mixed), channel_id=1, source_target_pairs={{0,8},{8,16},{16,24},{24,32},{32,40},{40,48},{48,56},{56,64},{64,7... | collective-permute-start | bytes 786440 | tf_op jit(solution)/shard_map/ppermute | solution.py:24
  5.4 0.0 copy-done
  5.4 0.0 copy-start.5
  5.4 2.4 %own.1 = f32[128,1024]{1,0:T(8,128)S(1)} custom-call(bf16[128,1024]{1,0:T(8,128)(2,1)S(1)} %multiply_convert_fusion.mixed, f32[128,1024]{1,0:T(8,128)S(1)} %copy-done), custom_call_target="tpu_custom_call" | custom-call | flops 16777216 | bytes 1310720 | tf_op jit(solution)/shard_map/own/pallas_call | solution.py:36
  7.8 13.0 %collective-permute-done.earlier = bf16[128,1024]{1,0:T(8,128)(2,1)S(1)} collective-permute-done((bf16[128,1024]{1,0:T(8,128)(2,1)S(1)}, bf16[128,1024]{1,0:T(8,128)(2,1)S(1)}, u32[]{:S(2)}, u32[]{:S(2)}) %collective-permute-start) | collective-permute-done | bytes 262176 | tf_op jit(solution)/shard_map/ppermute | solution.py:24
  20.7 0.0 copy-done.1
  20.7 2.8 %rim.1 = (f32[128,1024]{1,0:T(8,128)S(1)}, f32[8,8,128]{2,1,0:T(8,128)S(1)}) custom-call(f32[128,1024]{1,0:T(8,128)S(1)} %own.1, bf16[128,1024]{1,0:T(8,128)(2,1)S(1)} %collective-permute-done.earlier, f32[128,1024]{1,0:T(8,128)S(1)} %copy-done, bf16[128,1024]{1,0:T(8,128)(2,1)S(1)} %copy-done.1, bf16[128,1024]{1,0:T(8,128)(2,1)S(1)} %copy-done.2, ...), custom_call_target="tpu_custom_call" | custom-call | flops 16777216 | bytes 2396160 | tf_op jit(solution)/shard_map/rim/pallas_call | solution.py:36
  23.5 7.8 %all_to_all.20.sums = f32[8,8,128]{2,1,0:T(8,128)S(1)} all-to-all(f32[8,8,128]{2,1,0:T(8,128)S(1)} %get-tuple-element.18), channel_id=1, replica_groups=mesh['zh'=8,'zl'=4,'x'=4,'tp'=8] {'tp'}, dimensions={0} | all-to-all | bytes 65536 | tf_op jit(solution)/shard_map/all_to_all | solution.py:230
  31.3 5.7 %grads.1 = (bf16[128,1024]{1,0:T(8,128)(2,1)S(1)}, bf16[128,1024]{1,0:T(8,128)(2,1)}, bf16[128,1152]{1,0:T(8,128)(2,1)S(1)}) custom-call(f32[8,8,128]{2,1,0:T(8,128)S(1)} %all_to_all.20.sums, f32[128,1024]{1,0:T(8,128)S(1)} %get-tuple-element.19.conv, bf16[128,1024]{1,0:T(8,128)(2,1)S(1)} %copy-done.1, bf16[128,1024]{1,0:T(8,128)(2,1)S(1)} %copy-done.2, ...), custom_call_target="tpu_custom_call" | custom-call | flops 33554432 | bytes 2428928 | tf_op jit(solution)/shard_map/grads/pallas_call | solution.py:36
  37.0 12.9 %all_to_all.21 = bf16[16,8,1152]{2,1,0:T(8,128)(2,1)S(1)} all-to-all(bf16[16,8,1152]{2,1,0:T(8,128)(2,1)S(1)} %bitcast.5), channel_id=1, replica_groups=mesh['zh'=8,'zl'=4,'x'=4,'tp'=8] {'zl','x'}, dimensions={0} | all-to-all | bytes 589824 | tf_op jit(solution)/shard_map/all_to_all | solution.py:247
  49.9 0.0 copy-start.3
  49.9 0.7 broadcast_in_dim.4
  50.6 25.0 %all-to-all-start.2 = ((bf16[8,8,1152]{2,1,0:T(8,128)(2,1)}), bf16[8,8,1152]{2,1,0:T(8,128)(2,1)S(1)}, u32[]{:S(2)}, u32[]{:S(2)}) async-start(bf16[8,8,1152]{2,1,0:T(8,128)(2,1)} %broadcast_in_dim.4), calls=%async_computation.2 | async-start | bytes 294912 | tf_op jit(solution)/shard_map/all_to_all | solution.py:30
  75.6 3.4 %collective-permute-start.1 = (bf16[128,1024]{1,0:T(8,128)(2,1)S(1)}, bf16[128,1024]{1,0:T(8,128)(2,1)S(1)}, u32[]{:S(2)}, u32[]{:S(2)}) collective-permute-start(bf16[128,1024]{1,0:T(8,128)(2,1)S(1)} %get-tuple-element.24.grad_conv), channel_id=1, source_target_pairs={{8,0},{16,8},{24,16},{32,24},{40,32},{48,40},{56,48},{64,56},{72,6... | collective-permute-start | bytes 786440 | tf_op jit(solution)/shard_map/ppermute | solution.py:24
  78.9 5.1 %collective-permute-done.1.later = bf16[128,1024]{1,0:T(8,128)(2,1)S(1)} collective-permute-done((bf16[128,1024]{1,0:T(8,128)(2,1)S(1)}, bf16[128,1024]{1,0:T(8,128)(2,1)S(1)}, u32[]{:S(2)}, u32[]{:S(2)}) %collective-permute-start.1) | collective-permute-done | bytes 262176 | tf_op jit(solution)/shard_map/ppermute | solution.py:24
  84.1 0.0 copy-done.4
  84.1 5.4 %back.1 = (bf16[128,1024]{1,0:T(8,128)(2,1)}, bf16[128,1024]{1,0:T(8,128)(2,1)}) custom-call(bf16[128,1024]{1,0:T(8,128)(2,1)S(1)} %get-tuple-element.24.grad_conv, bf16[128,1024]{1,0:T(8,128)(2,1)S(1)} %collective-permute-done.1.later, f32[128,1024]{1,0:T(8,128)S(1)} %copy-done, bf16[128,1024]{1,0:T(8,128)(2,1)S(1)} %copy-done.4, ...), custom_call_target="tpu_custom_call" | custom-call | flops 33554432 | bytes 2097152 | tf_op jit(solution)/shard_map/back/pallas_call | solution.py:36
  89.5 14.9 %all-to-all-done.2 = bf16[8,8,1152]{2,1,0:T(8,128)(2,1)S(1)} async-done(((bf16[8,8,1152]{2,1,0:T(8,128)(2,1)}), bf16[8,8,1152]{2,1,0:T(8,128)(2,1)S(1)}, u32[]{:S(2)}, u32[]{:S(2)}) %all-to-all-start.2) | async-done | bytes 147488 | tf_op jit(solution)/shard_map/all_to_all | solution.py:30
  104.5 15.2 %all_to_all.22 = bf16[16,8,1152]{2,1,0:T(8,128)(2,1)S(1)} all-to-all(bf16[16,8,1152]{2,1,0:T(8,128)(2,1)S(1)} %broadcast_in_dim.5), channel_id=1, replica_groups=mesh['zh'=8,'zl'=4,'x'=4,'tp'=8] {'zl','x'}, dimensions={0} | all-to-all | bytes 589824 | tf_op jit(solution)/shard_map/all_to_all | solution.py:30
  119.7 0.8 final.1
  (7 shorter events, 0.1 us)
Async XLA Ops:
  0.6 4.7 %copy-start = (f32[128,1024]{1,0:T(8,128)S(1)}, f32[128,1024]{1,0:T(8,128)}, u32[]{:S(2)}) copy-start(f32[128,1024]{1,0:T(8,128)} %filters.5) | copy-start | bytes 1572868
  1.8 18.9 %copy-start.1 = (bf16[128,1024]{1,0:T(8,128)(2,1)S(1)}, bf16[128,1024]{1,0:T(8,128)(2,1)}, u32[]{:S(2)}) copy-start(bf16[128,1024]{1,0:T(8,128)(2,1)} %query.3) | copy-start | bytes 786436
  1.8 18.9 %copy-start.2 = (bf16[128,1024]{1,0:T(8,128)(2,1)S(1)}, bf16[128,1024]{1,0:T(8,128)(2,1)}, u32[]{:S(2)}) copy-start(bf16[128,1024]{1,0:T(8,128)(2,1)} %cot.3) | copy-start | bytes 786436
  1.8 18.9 %collective-permute-start = (bf16[128,1024]{1,0:T(8,128)(2,1)S(1)}, bf16[128,1024]{1,0:T(8,128)(2,1)S(1)}, u32[]{:S(2)}, u32[]{:S(2)}) collective-permute-start(bf16[128,1024]{1,0:T(8,128)(2,1)S(1)} %multiply_convert_fusion.mixed), channel_id=1, source_target_pairs={{0,8},{8,16},{16,24},{24,32},{32,40},{40,48},{48,56},{56,64},{64,7... | collective-permute-start | bytes 786440 | tf_op jit(solution)/shard_map/ppermute | solution.py:24
  5.4 15.4 %copy-start.5 = (f32[1024]{0:T(1024)S(1)}, f32[1024]{0:T(1024)}, u32[]{:S(2)}) copy-start(f32[1024]{0:T(1024)} %param.11) | copy-start | bytes 12292
  49.9 34.2 %copy-start.4 = (bf16[128,1024]{1,0:T(8,128)(2,1)S(1)}, bf16[128,1024]{1,0:T(8,128)(2,1)}, u32[]{:S(2)}) copy-start(bf16[128,1024]{1,0:T(8,128)(2,1)} %k_proj.1) | copy-start | bytes 786436
  49.9 34.2 %copy-start.3 = (bf16[128,1024]{1,0:T(8,128)(2,1)S(1)}, bf16[128,1024]{1,0:T(8,128)(2,1)}, u32[]{:S(2)}) copy-start(bf16[128,1024]{1,0:T(8,128)(2,1)} %v_proj.1) | copy-start | bytes 786436
  50.6 53.8 %all-to-all-start.2 = ((bf16[8,8,1152]{2,1,0:T(8,128)(2,1)}), bf16[8,8,1152]{2,1,0:T(8,128)(2,1)S(1)}, u32[]{:S(2)}, u32[]{:S(2)}) async-start(bf16[8,8,1152]{2,1,0:T(8,128)(2,1)} %broadcast_in_dim.4), calls=%async_computation.2 | async-start | bytes 294912 | tf_op jit(solution)/shard_map/all_to_all | solution.py:30
  75.6 8.5 %collective-permute-start.1 = (bf16[128,1024]{1,0:T(8,128)(2,1)S(1)}, bf16[128,1024]{1,0:T(8,128)(2,1)S(1)}, u32[]{:S(2)}, u32[]{:S(2)}) collective-permute-start(bf16[128,1024]{1,0:T(8,128)(2,1)S(1)} %get-tuple-element.24.grad_conv), channel_id=1, source_target_pairs={{8,0},{16,8},{24,16},{32,24},{40,32},{48,40},{56,48},{64,56},{72,6... | collective-permute-start | bytes 786440 | tf_op jit(solution)/shard_map/ppermute | solution.py:24

commit v3 on v2

--- a/solution.py
+++ b/solution.py
@@ -133,16 +133,12 @@
     return parts[0]
 
 
-def grads_kernel(
-    sums, conv, query, cot, gain, earlier, mixed, grad_conv, grad_q, block, window, inverse, pull, partial
-):
+def grads_kernel(sums, conv, query, cot, gain, grad_conv, grad_q, gains, inverse, pull):
     rows, width = conv.shape
-    count = rows // SUB
     both = jnp.sum(sums[...], 0)
     rms = jnp.sqrt(both[0:1] / D + epsilon)
     inverse[...] = jnp.broadcast_to(1.0 / rms, (LANES, rows)).T
     pull[...] = jnp.broadcast_to(both[1:2] / (D * (rms * rms * rms)), (LANES, rows)).T
-    block[:, width:] = jnp.zeros((rows, LANES), bf16)
 
     def tile(index, lanes):
         whole = conv[:, lanes]
@@ -150,14 +146,24 @@
         cot_f32 = cot[:, lanes].astype(f32)
         product = query_f32 * whole
         grad_product = gain[:, lanes] * cot_f32 * inverse[...] - product * pull[...]
-        rounded = (query_f32 * grad_product).astype(bf16)
-        grad_conv[:, lanes] = rounded
+        grad_conv[:, lanes] = (query_f32 * grad_product).astype(bf16)
         grad_q[:, lanes] = (grad_product * whole).astype(bf16)
-        gains = jnp.sum((cot_f32 * product * inverse[...]).reshape(count, SUB, LANES), 0)
-        block[pl.ds(pl.multiple_of(index * SUB, SUB), SUB), width:] = gains.astype(bf16)
+        parts = (cot_f32 * product * inverse[...]).reshape(rows // SUB, SUB, LANES)
+        gains[pl.ds(pl.multiple_of(index * SUB, SUB), SUB), :] = jnp.sum(parts, 0).astype(bf16)
+
+    over_tiles(width, tile)
+
+
+def taps_kernel(grad_conv, gains, earlier, mixed, block, window, partial):
+    rows, width = grad_conv.shape
+    count = rows // SUB
+    block[:, width:] = jnp.zeros((rows, LANES), bf16)
+    block[pl.ds(0, gains.shape[0]), width:] = gains[...]
+
+    def tile(_, lanes):
         fill(window, 0, earlier[:, lanes])
         fill(window, rows, mixed[:, lanes])
-        ours = blocks(rounded.astype(f32))
+        ours = blocks(grad_conv[:, lanes].astype(f32))
         for shift in range(SUB):
             slid = [window[pl.ds(SUB * (i + 1) - shift, SUB), :] for i in range(2 * count - 1)]
             for step in range(count):
@@ -228,27 +234,37 @@
         flops=macs // 2,
     )
     sums = lax.all_to_all(sums, "tp", 0, 0)
-    grad_conv, grad_q, block = call(
+    grad_conv, grad_q, gains = call(
         grads_kernel,
-        (struct((rows, width), bf16), struct((rows, width), bf16), struct((rows, width + LANES), bf16)),
+        (struct((rows, width), bf16), struct((rows, width), bf16), struct((width // LANES * SUB, LANES), bf16)),
         sums,
         conv,
         q_proj,
         cotangent,
         gain,
+        scratch=(tile, tile),
+        name="grads",
+        flops=rows * width * 12,
+    )
+    later = passed_along(grad_conv, -1)
+    (block,) = call(
+        taps_kernel,
+        (struct((rows, width + LANES), bf16),),
+        grad_conv,
+        gains,
         earlier,
         mixed,
-        scratch=(long, tile, tile, pltpu.VMEM((rows, SUB, LANES), f32)),
-        name="grads",
+        scratch=(long, pltpu.VMEM((rows, SUB, LANES), f32)),
+        name="taps",
         flops=macs,
     )
+    block, later = lax.optimization_barrier((block, later))
     near = lax.axis_size(NEAR)
     block = block.reshape(near, rows // near, width + LANES)
     block = lax.all_to_all(block, NEAR, 0, 0)
     block = jnp.sum(block.astype(f32), 0).astype(bf16)
-    block, grad_conv = lax.optimization_barrier((block, grad_conv))
+    block, grad_conv, later = lax.optimization_barrier((block, grad_conv, later))
     block = shared(block, FAR)
-    later = passed_along(grad_conv, -1)
     grad_k, grad_v = call(
         back_kernel,
         (struct((rows, width), bf16), struct((rows, width), bf16)),

time: 121 us -> 127 us (1.050)
  waiting for transfers between devices: 33 us -> 39.4 us
  starting transfers between devices: 31.9 us -> 29.5 us
  blocking collectives: 35.9 us -> 37.6 us
    all_to_all x1, waiting for transfers between devices: 14.9 us -> 23.5 us  [shared(): return lax.all_to_all(copies, axes, 0, 0)]
    all_to_all x1, blocking collectives: 12.9 us -> 15.3 us  [shards(): block = lax.all_to_all(block, NEAR, 0, 0)]
    ppermute x2, waiting for transfers between devices: 18.1 us -> 15.9 us  [passed_along(): return lax.ppermute(value, CTX, pairs)]
    ppermute x2, starting transfers between devices: 6.88 us -> 5.44 us  [passed_along(): return lax.ppermute(value, CTX, pairs)]
    pallas_call x5 -> x6, Pallas kernels: 17 us -> 17.7 us  [call(): pl.pallas_call(kernel, out_shape=outs, in_specs=[in_vmem] * len(operands)...]
  transfers between devices with their start and end apart: 3 -> 3, of which waited for: 3 -> 3; matrix products, arithmetic and copies ran while one was open for 0% -> 0% of each run, Pallas kernels for 6% -> 10%
where the time goes in v3:
time: 127 us
  waiting for transfers between devices  39.4 us (31%)
  blocking collectives  37.6 us (30%)
  starting transfers between devices  29.5 us (23%)
  Pallas kernels  17.7 us (14%)
    all_to_all x1, starting transfers between devices, shared(): return lax.all_to_all(copies, axes, 0, 0)  24.1 us
    all_to_all x1, waiting for transfers between devices, shared(): return lax.all_to_all(copies, axes, 0, 0)  23.5 us
    pallas_call x6, Pallas kernels, call(): pl.pallas_call(kernel, out_shape=outs, in_specs=[in_vmem] * len(operands)...  17.7 us
    ppermute x2, waiting for transfers between devices, passed_along(): return lax.ppermute(value, CTX, pairs)  15.9 us
    all_to_all x1, blocking collectives, shards(): block = lax.all_to_all(block, NEAR, 0, 0)  15.3 us
    all_to_all x1, blocking collectives, shared(): return lax.all_to_all(copies, axes, 0, 0)  14.4 us
    all_to_all x1, blocking collectives, shards(): sums = lax.all_to_all(sums, 'tp', 0, 0)  7.82 us
    ppermute x2, starting transfers between devices, passed_along(): return lax.ppermute(value, CTX, pairs)  5.44 us
  transfers between devices with their start and end apart: 3, of which 3 were waited for; matrix products, arithmetic and copies ran while one was open for 0% of the time, Pallas kernels for 10%

profile of v3, /device:TPU:2, one launch (start us, length us, event | category | flops | bytes accessed | tf_op | source)
XLA Modules:
  0.0 126.8 jit_solution(1346866390133582401)
XLA Ops:
  0.6 0.0 copy-start
  0.6 1.2 multiply_convert_fusion.mixed
  1.8 0.0 copy-start.1
  1.8 0.0 copy-start.2
  1.8 3.5 %collective-permute-start = (bf16[128,1024]{1,0:T(8,128)(2,1)S(1)}, bf16[128,1024]{1,0:T(8,128)(2,1)S(1)}, u32[]{:S(2)}, u32[]{:S(2)}) collective-permute-start(bf16[128,1024]{1,0:T(8,128)(2,1)S(1)} %multiply_convert_fusion.mixed), channel_id=1, source_target_pairs={{0,8},{8,16},{16,24},{24,32},{32,40},{40,48},{48,56},{56,64},{64,7... | collective-permute-start | bytes 786440 | tf_op jit(solution)/shard_map/ppermute | solution.py:24
  5.4 0.0 copy-done
  5.4 0.0 copy-start.5
  5.4 2.4 %own.1 = f32[128,1024]{1,0:T(8,128)S(1)} custom-call(bf16[128,1024]{1,0:T(8,128)(2,1)S(1)} %multiply_convert_fusion.mixed, f32[128,1024]{1,0:T(8,128)S(1)} %copy-done), custom_call_target="tpu_custom_call" | custom-call | flops 16777216 | bytes 1310720 | tf_op jit(solution)/shard_map/own/pallas_call | solution.py:36
  7.8 13.0 %collective-permute-done.earlier = bf16[128,1024]{1,0:T(8,128)(2,1)S(1)} collective-permute-done((bf16[128,1024]{1,0:T(8,128)(2,1)S(1)}, bf16[128,1024]{1,0:T(8,128)(2,1)S(1)}, u32[]{:S(2)}, u32[]{:S(2)}) %collective-permute-start) | collective-permute-done | bytes 262176 | tf_op jit(solution)/shard_map/ppermute | solution.py:24
  20.7 0.0 copy-done.1
  20.7 2.8 %rim.1 = (f32[128,1024]{1,0:T(8,128)S(1)}, f32[8,8,128]{2,1,0:T(8,128)S(1)}) custom-call(f32[128,1024]{1,0:T(8,128)S(1)} %own.1, bf16[128,1024]{1,0:T(8,128)(2,1)S(1)} %collective-permute-done.earlier, f32[128,1024]{1,0:T(8,128)S(1)} %copy-done, bf16[128,1024]{1,0:T(8,128)(2,1)S(1)} %copy-done.1, bf16[128,1024]{1,0:T(8,128)(2,1)S(1)} %copy-done.2, ...), custom_call_target="tpu_custom_call" | custom-call | flops 16777216 | bytes 2396160 | tf_op jit(solution)/shard_map/rim/pallas_call | solution.py:36
  23.5 7.8 %all_to_all.20.sums = f32[8,8,128]{2,1,0:T(8,128)S(1)} all-to-all(f32[8,8,128]{2,1,0:T(8,128)S(1)} %get-tuple-element.21), channel_id=1, replica_groups=mesh['zh'=8,'zl'=4,'x'=4,'tp'=8] {'tp'}, dimensions={0} | all-to-all | bytes 65536 | tf_op jit(solution)/shard_map/all_to_all | solution.py:236
  31.3 1.2 grads.1
  32.6 1.9 %collective-permute-start.1 = (bf16[128,1024]{1,0:T(8,128)(2,1)S(1)}, bf16[128,1024]{1,0:T(8,128)(2,1)S(1)}, u32[]{:S(2)}, u32[]{:S(2)}) collective-permute-start(bf16[128,1024]{1,0:T(8,128)(2,1)S(1)} %get-tuple-element.29.grad_conv), channel_id=1, source_target_pairs={{8,0},{16,8},{24,16},{32,24},{40,32},{48,40},{56,48},{64,56},{72,6... | collective-permute-start | bytes 786440 | tf_op jit(solution)/shard_map/ppermute | solution.py:24
  34.5 5.0 %taps.1 = bf16[128,1152]{1,0:T(8,128)(2,1)S(1)} custom-call(bf16[128,1024]{1,0:T(8,128)(2,1)S(1)} %get-tuple-element.29.grad_conv, bf16[64,128]{1,0:T(8,128)(2,1)S(1)} %get-tuple-element.25.gains, bf16[128,1024]{1,0:T(8,128)(2,1)S(1)} %collective-permute-done.earlier, bf16[128,1024]{1,0:T(8,128)(2,1)S(1)} %multiply_convert_fusion.mixed), custom_call_target="tpu_custom_call" | custom-call | flops 33554432 | bytes 1097728 | tf_op jit(solution)/shard_map/taps/pallas_call | solution.py:36
  39.5 2.9 %collective-permute-done.1.later = bf16[128,1024]{1,0:T(8,128)(2,1)S(1)} collective-permute-done((bf16[128,1024]{1,0:T(8,128)(2,1)S(1)}, bf16[128,1024]{1,0:T(8,128)(2,1)S(1)}, u32[]{:S(2)}, u32[]{:S(2)}) %collective-permute-start.1) | collective-permute-done | bytes 262176 | tf_op jit(solution)/shard_map/ppermute | solution.py:24
  42.4 15.3 %all_to_all.21 = bf16[16,8,1152]{2,1,0:T(8,128)(2,1)S(1)} all-to-all(bf16[16,8,1152]{2,1,0:T(8,128)(2,1)S(1)} %bitcast.5), channel_id=1, replica_groups=mesh['zh'=8,'zl'=4,'x'=4,'tp'=8] {'zl','x'}, dimensions={0} | all-to-all | bytes 589824 | tf_op jit(solution)/shard_map/all_to_all | solution.py:264
  57.8 0.0 copy-start.3
  57.8 0.7 broadcast_in_dim.4
  58.5 24.1 %all-to-all-start.2 = ((bf16[8,8,1152]{2,1,0:T(8,128)(2,1)}), bf16[8,8,1152]{2,1,0:T(8,128)(2,1)S(1)}, u32[]{:S(2)}, u32[]{:S(2)}) async-start(bf16[8,8,1152]{2,1,0:T(8,128)(2,1)} %broadcast_in_dim.4), calls=%async_computation.2 | async-start | bytes 294912 | tf_op jit(solution)/shard_map/all_to_all | solution.py:30
  82.6 5.4 %back.1 = (bf16[128,1024]{1,0:T(8,128)(2,1)}, bf16[128,1024]{1,0:T(8,128)(2,1)}) custom-call(bf16[128,1024]{1,0:T(8,128)(2,1)S(1)} %get-tuple-element.29.grad_conv, bf16[128,1024]{1,0:T(8,128)(2,1)S(1)} %collective-permute-done.1.later, f32[128,1024]{1,0:T(8,128)S(1)} %copy-done, bf16[128,1024]{1,0:T(8,128)(2,1)S(1)} %copy-done.4, ...), custom_call_target="tpu_custom_call" | custom-call | flops 33554432 | bytes 2097152 | tf_op jit(solution)/shard_map/back/pallas_call | solution.py:36
  88.0 23.5 %all-to-all-done.2 = bf16[8,8,1152]{2,1,0:T(8,128)(2,1)S(1)} async-done(((bf16[8,8,1152]{2,1,0:T(8,128)(2,1)}), bf16[8,8,1152]{2,1,0:T(8,128)(2,1)S(1)}, u32[]{:S(2)}, u32[]{:S(2)}) %all-to-all-start.2) | async-done | bytes 147488 | tf_op jit(solution)/shard_map/all_to_all | solution.py:30
  111.6 14.4 %all_to_all.22 = bf16[16,8,1152]{2,1,0:T(8,128)(2,1)S(1)} all-to-all(bf16[16,8,1152]{2,1,0:T(8,128)(2,1)S(1)} %broadcast_in_dim.5), channel_id=1, replica_groups=mesh['zh'=8,'zl'=4,'x'=4,'tp'=8] {'zl','x'}, dimensions={0} | all-to-all | bytes 589824 | tf_op jit(solution)/shard_map/all_to_all | solution.py:30
  126.0 0.8 final.1
  (8 shorter events, 0.1 us)
Async XLA Ops:
  0.6 4.7 %copy-start = (f32[128,1024]{1,0:T(8,128)S(1)}, f32[128,1024]{1,0:T(8,128)}, u32[]{:S(2)}) copy-start(f32[128,1024]{1,0:T(8,128)} %filters.5) | copy-start | bytes 1572868
  1.8 18.9 %copy-start.1 = (bf16[128,1024]{1,0:T(8,128)(2,1)S(1)}, bf16[128,1024]{1,0:T(8,128)(2,1)}, u32[]{:S(2)}) copy-start(bf16[128,1024]{1,0:T(8,128)(2,1)} %query.3) | copy-start | bytes 786436
  1.8 18.9 %copy-start.2 = (bf16[128,1024]{1,0:T(8,128)(2,1)S(1)}, bf16[128,1024]{1,0:T(8,128)(2,1)}, u32[]{:S(2)}) copy-start(bf16[128,1024]{1,0:T(8,128)(2,1)} %cot.3) | copy-start | bytes 786436
  1.8 18.9 %collective-permute-start = (bf16[128,1024]{1,0:T(8,128)(2,1)S(1)}, bf16[128,1024]{1,0:T(8,128)(2,1)S(1)}, u32[]{:S(2)}, u32[]{:S(2)}) collective-permute-start(bf16[128,1024]{1,0:T(8,128)(2,1)S(1)} %multiply_convert_fusion.mixed), channel_id=1, source_target_pairs={{0,8},{8,16},{16,24},{24,32},{32,40},{40,48},{48,56},{56,64},{64,7... | collective-permute-start | bytes 786440 | tf_op jit(solution)/shard_map/ppermute | solution.py:24
  5.4 15.4 %copy-start.5 = (f32[1024]{0:T(1024)S(1)}, f32[1024]{0:T(1024)}, u32[]{:S(2)}) copy-start(f32[1024]{0:T(1024)} %param.11) | copy-start | bytes 12292
  32.6 9.9 %collective-permute-start.1 = (bf16[128,1024]{1,0:T(8,128)(2,1)S(1)}, bf16[128,1024]{1,0:T(8,128)(2,1)S(1)}, u32[]{:S(2)}, u32[]{:S(2)}) collective-permute-start(bf16[128,1024]{1,0:T(8,128)(2,1)S(1)} %get-tuple-element.29.grad_conv), channel_id=1, source_target_pairs={{8,0},{16,8},{24,16},{32,24},{40,32},{48,40},{56,48},{64,56},{72,6... | collective-permute-start | bytes 786440 | tf_op jit(solution)/shard_map/ppermute | solution.py:24
  57.7 24.8 %copy-start.4 = (bf16[128,1024]{1,0:T(8,128)(2,1)S(1)}, bf16[128,1024]{1,0:T(8,128)(2,1)}, u32[]{:S(2)}) copy-start(bf16[128,1024]{1,0:T(8,128)(2,1)} %k_proj.1) | copy-start | bytes 786436
  57.8 24.7 %copy-start.3 = (bf16[128,1024]{1,0:T(8,128)(2,1)S(1)}, bf16[128,1024]{1,0:T(8,128)(2,1)}, u32[]{:S(2)}) copy-start(bf16[128,1024]{1,0:T(8,128)(2,1)} %v_proj.1) | copy-start | bytes 786436
  58.5 53.0 %all-to-all-start.2 = ((bf16[8,8,1152]{2,1,0:T(8,128)(2,1)}), bf16[8,8,1152]{2,1,0:T(8,128)(2,1)S(1)}, u32[]{:S(2)}, u32[]{:S(2)}) async-start(bf16[8,8,1152]{2,1,0:T(8,128)(2,1)} %broadcast_in_dim.4), calls=%async_computation.2 | async-start | bytes 294912 | tf_op jit(solution)/shard_map/all_to_all | solution.py:30
